TPU v7x, 32 devices: a whole 2x2x4 slice. The times are simulated.
32 devices in a mesh: grp: 2 (over y), garm: 4 (over z), body: 2 (over x), frame: 2 (over core).
Axes of the slice: x: 2, y: 2, z: 4, core: 2. Of those that a mesh axis runs over, the one named last changes fastest.
Arguments:
- garment: float32 [4, 3, 32768], P(('grp', 'frame'), None, ('garm', 'body')), parts along dimension 0, may hold values from -6 to 6
- cotangent: float32 [4, 32768], P(('grp', 'frame'), ('garm', 'body')), parts along dimension 0, may hold values from -6 to 6
- body_points: float32 [4, 3, 16384], P(('grp', 'frame'), None, ('garm', 'body')), parts along dimension 0, may hold values from -6 to 6
- stiffness: float32 [32768], P(('grp', 'garm', 'body')), parts along dimension 0, may hold values from 0.2 to 2
- pair_garment: int32 [4, 8, 8, 4], P(('grp', 'frame'), ('garm', 'body')), parts along dimension 0, may hold values from 0 to 31
- pair_body: int32 [4, 8, 8, 4], P(('grp', 'frame'), ('garm', 'body')), parts along dimension 0, may hold values from 0 to 15
- pair_count: int32 [4, 8, 8], P(('grp', 'frame'), ('garm', 'body')), parts along dimension 0, may hold values from 0 to 4, as said below
Outputs:
- garment_grad: float32 [4, 3, 32768], P(('grp', 'frame'), None, ('garm', 'body')), parts along dimension 0
- body_grad: float32 [4, 3, 16384], P(('grp', 'frame'), None, ('garm', 'body')), parts along dimension 0
- stiffness_grad: float32 [32768], P(('grp', 'garm', 'body')), parts along dimension 0
There are 2 independent parts, one for each index of `grp`. A program takes and returns all parts, laid end to end along the dimension named above; each array names one. Nothing has to cross between parts.
Inputs may be any that keep to these rules, and one draw needn't show every extreme that they name: pair_count gives the live slots; in every frame one receiving owner gets 4 live slots from every sending owner. `pair_garment`: slots at or past the count are unused and hold arbitrary block numbers. `pair_body`: slots at or past the count are unused and hold arbitrary block numbers.
All inputs are finite; a program needn't handle non-finite values.
Results may differ from a plain program's by a relative error of at most 0.00016.
Values sent between devices are 32-bit elements; how exact they have to be, the bound alone decides.
A program may use at most 64 MiB of HBM per device.

v0:
```python
import functools
import math

import jax
import jax.numpy as jnp
from jax import lax
from jax.experimental import pallas as pl
from jax.experimental.pallas import tpu as pltpu
from jax.sharding import PartitionSpec as P

BLOCK = 128
amplitude = 0.05
width_sq = 4.0
SCALE = math.sqrt(math.log2(math.e) / width_sq)
GRAD = -2.0 / width_sq * amplitude / SCALE
GROUP = 8
MESH = pl.DeviceIdType.MESH
BF = jnp.bfloat16
F32 = jnp.float32


def split3(v):
    hi = v.astype(BF)
    rest = v - hi.astype(F32)
    mid = rest.astype(BF)
    return hi, mid, (rest - mid.astype(F32)).astype(BF)


def dot(a, b):
    return jnp.dot(a, b, preferred_element_type=F32)


def dot_t(a, b):
    return lax.dot_general(a, b, (((1,), (1,)), ((), ())), preferred_element_type=F32)


def each(count, body):
    if count <= 8:
        for k in range(count):
            body(k)
    else:
        lax.fori_loop(0, count, lambda k, c: (body(k), c)[1], 0)


def kernel(owners, inner, cap, gb, bb, *refs):
    hbm, refs = refs[:7], refs[7:]
    (out_g, out_b, out_s, garm, cot, body, stiff, pg, pb, pc, isem, k_his, k_los, weights, bodies,
     send, recv, rsend, rrecv, tab3, gtgt, parts, stl, strv,
     ssem, rsem, rssem, rrsem, fsem) = refs
    rows = 4 * cap
    outer_i, inner_i, frame_i = lax.axis_index("garm"), lax.axis_index("body"), lax.axis_index("frame")
    me = outer_i * inner + inner_i

    def peer(k):
        p, bit = me, 1
        while bit < owners:
            p = p + ((k // bit) % 2) * (bit - 2 * bit * ((me // bit) % 2))
            bit *= 2
        return p

    def device(k):
        p = peer(k)
        return {"garm": p // inner, "body": p % inner}

    barrier = pltpu.get_barrier_semaphore()

    def greet(j):
        pl.semaphore_signal(barrier, inc=1, device_id=device(owners - 1 - j), device_id_type=MESH)

    loads = [
        pltpu.make_async_copy(src, dst, isem.at[i])
        for i, (src, dst) in enumerate(zip(hbm, (garm, cot, body, stiff, pg, pb, pc)))]
    for load in loads:
        load.start()
    each(owners - 1, greet)
    pl.semaphore_signal(barrier, inc=1, device_id={"frame": 1 - frame_i}, device_id_type=MESH)

    for load in loads:
        load.wait()

    lane = lax.broadcasted_iota(jnp.int32, (1, BLOCK), 1)
    lane_q = lane % rows // cap
    spread_row = lax.broadcasted_iota(jnp.int32, (16, 3 * BLOCK), 0)
    spread_lane = lax.broadcasted_iota(jnp.int32, (16, 3 * BLOCK), 1)
    spread_at = jnp.where(
        spread_lane < 2 * BLOCK, spread_lane // BLOCK * cap + spread_lane % cap, 2 * cap)
    spread = jnp.where(spread_row == spread_at, 1.0, 0.0).astype(BF)
    lists = jnp.concatenate(
        [pg[...], pb[...], pc[...], jnp.zeros((15 - 2 * cap, owners), jnp.int32)], axis=0)
    full = lax.dot_general(
        jnp.transpose(lists.astype(F32)).astype(BF), spread, (((1,), (0,)), ((), ())),
        preferred_element_type=F32)
    full_g = full[:, :BLOCK] + (lane_q * gb).astype(F32)
    full_b = full[:, BLOCK : 2 * BLOCK] + (lane_q * bb).astype(F32)
    live = jnp.where(
        (lane_q < 3) | ((lane % cap).astype(F32) < full[:, 2 * BLOCK :]), 1.0, 0.0)
    gtab = jnp.concatenate(
        split3(jnp.concatenate([garm[...] * SCALE, cot[...]], axis=0)), axis=0)
    own = lax.broadcasted_iota(jnp.int32, (GROUP, BLOCK), 0) == lane // rows
    wide_g = lax.broadcasted_iota(jnp.int32, (BLOCK, 12 * gb), 1) % (4 * gb)
    for u in range(owners // GROUP):
        here = slice(u * GROUP, (u + 1) * GROUP)
        targets = jnp.sum(jnp.where(own, full_g[here], 0.0), axis=0, keepdims=True)
        lives = jnp.sum(jnp.where(own, live[here], 0.0), axis=0, keepdims=True)
        gtgt[u] = targets
        turned = jnp.transpose(
            jnp.concatenate([targets, lives, jnp.zeros((6, BLOCK), F32)], axis=0))
        hot = jnp.where(wide_g == turned[:, 0:1].astype(jnp.int32), 1.0, 0.0).astype(BF)
        chosen = dot(hot, gtab) * turned[:, 1:2]
        for m in range(GROUP):
            send[u * GROUP + m, pl.ds(0, rows), :] = chosen[m * rows : (m + 1) * rows]
    for d in range(owners):
        send[d, pl.ds(rows, 1), :] = full_b[d : d + 1]

    def outgoing(k):
        return pltpu.make_async_remote_copy(
            src_ref=send.at[peer(k)], dst_ref=recv.at[me], send_sem=ssem.at[k], recv_sem=rsem.at[k],
            device_id=device(k), device_id_type=MESH)

    def returning(k):
        return pltpu.make_async_remote_copy(
            src_ref=rsend.at[peer(k)], dst_ref=rrecv.at[me], send_sem=rssem.at[k], recv_sem=rrsem.at[k],
            device_id=device(k), device_id_type=MESH)

    tab3[...] = jnp.concatenate(
        split3(jnp.concatenate([body[...] * SCALE, stiff[...]], axis=0)), axis=0)

    row_c = lax.broadcasted_iota(jnp.int32, (rows, BLOCK), 0) % cap
    low_i, low_j = row_c < 2, row_c % 2 == 0
    wide = lax.broadcasted_iota(jnp.int32, (rows, 3 * 4 * bb), 1) % (4 * bb)

    def lhs(x, low):
        both = jnp.concatenate([jnp.where(low, x, 0.0), jnp.where(low, 0.0, x)], axis=1)
        return jnp.concatenate(split3(both), axis=0)

    def process(k, got, row):
        turned = jnp.transpose(jnp.concatenate([got, row, jnp.zeros((7, BLOCK), F32)], axis=0))
        target = turned[:rows, rows : rows + 1]
        onehot = jnp.where(wide == target.astype(jnp.int32), 1.0, 0.0).astype(BF)
        part = dot(onehot, tab3[...])
        kernels = []
        for c in range(cap):
            dist = None
            for q in range(3):
                r = q * cap + c
                delta = turned[:, r : r + 1] - part[r : r + 1, :]
                dist = delta * delta if dist is None else dist + delta * delta
            kernels.append(jnp.exp2(-dist))
        square = jnp.concatenate(
            [jnp.concatenate(kernels[0:2], axis=1), jnp.concatenate(kernels[2:4], axis=1)], axis=0)
        k_hi = square.astype(BF)
        k_lo = (square - k_hi.astype(F32)).astype(BF)
        cots = got[3 * cap :]
        stf = part[3 * cap :]
        w = jnp.concatenate([jnp.concatenate([cots] * 3, axis=0) * got[: 3 * cap], cots], axis=0)
        v = jnp.concatenate([jnp.concatenate([stf] * 3, axis=0) * part[: 3 * cap], stf], axis=0)

        k_his[k], k_los[k] = k_hi, k_lo
        weights[k] = w
        bodies[k] = part
        lv = lhs(v, low_j)
        rg = dot_t(lv, k_hi) + dot_t(lv, k_lo)
        rg = rg[:rows] + rg[rows : 2 * rows] + rg[2 * rows :]
        rg = jnp.where(low_i, rg[:, :BLOCK], rg[:, BLOCK:])
        sums = jnp.concatenate([rg[3 * cap :]] * 3, axis=0)
        cots3 = jnp.concatenate([cots] * 3, axis=0)
        return GRAD * (cots3 * (got[: 3 * cap] * sums - rg[: 3 * cap]))

    def finish(k):
        part = bodies[k]
        lw = lhs(weights[k], low_i)
        rb = dot(lw, k_his[k]) + dot(lw, k_los[k])
        rb = rb[:rows] + rb[rows : 2 * rows] + rb[2 * rows :]
        rb = jnp.where(low_j, rb[:, :BLOCK], rb[:, BLOCK:])
        cols = rb[3 * cap :]
        cols3 = jnp.concatenate([cols] * 3, axis=0)
        stf3 = jnp.concatenate([part[3 * cap :]] * 3, axis=0)
        body_grad = GRAD * (stf3 * (part[: 3 * cap] * cols3 - rb[: 3 * cap]))
        parts[k] = jnp.concatenate([body_grad, amplitude * cols], axis=0)

    recv[me, pl.ds(rows, 1), :] = send[me, pl.ds(rows, 1), :]
    rrecv[me] = process(me, send[me, pl.ds(0, rows), :], send[me, pl.ds(rows, 1), :])

    pl.semaphore_wait(barrier, owners)
    each(owners - 1, lambda j: outgoing(owners - 1 - j).start())


    def arrive(ks):
        for k in ks:
            outgoing(k).wait_recv()
        grads = [process(peer(k), recv[peer(k), pl.ds(0, rows), :], recv[peer(k), pl.ds(rows, 1), :])
                 for k in ks]
        for k, grad in zip(ks, grads):
            rsend[peer(k)] = grad
            returning(k).start()

    arrive([1])
    each(owners // 2 - 1, lambda j: arrive([2 * j + 2, 2 * j + 3]))
    each(owners, finish)

    def scatter(height, target_row, values):
        hot = jnp.where(
            lax.broadcasted_iota(jnp.int32, (height, BLOCK), 0) == target_row, 1.0, 0.0).astype(BF)
        hi, mid, lo = split3(values)
        return dot(jnp.concatenate([hot, hot, hot], axis=1), jnp.concatenate([hi, mid, lo], axis=0))

    def over_groups(one):
        total = one(0)
        for u in range(1, owners // GROUP):
            total = total + one(u)
        return total

    def body_group(u):
        target = jnp.zeros((1, BLOCK), F32)
        for m in range(GROUP):
            target = jnp.where(lane // rows == m, recv[u * GROUP + m, pl.ds(rows, 1), :], target)
        return scatter(4 * bb, target.astype(jnp.int32),
                       jnp.concatenate([parts[u * GROUP + m] for m in range(GROUP)], axis=0))

    body_sum = over_groups(body_group)
    stl[...] = body_sum[3 * bb :]
    stiff_copy = pltpu.make_async_remote_copy(
        src_ref=stl, dst_ref=strv, send_sem=fsem.at[0], recv_sem=fsem.at[1],
        device_id={"frame": 1 - frame_i}, device_id_type=MESH)
    stiff_copy.start()
    out_b[...] = body_sum[: 3 * bb]
    each(owners - 1, lambda j: outgoing(j + 1).wait_send())
    stiff_copy.wait()
    out_s[...] = stl[...] + strv[...]
    each(owners - 1, lambda j: returning(j + 1).wait_recv())

    def garm_group(u):
        blank = jnp.zeros((cap, BLOCK), F32)
        pieces = []
        for m in range(GROUP):
            pieces += [rrecv[u * GROUP + m], blank]
        return scatter(3 * gb, gtgt[u].astype(jnp.int32), jnp.concatenate(pieces, axis=0))

    out_g[...] = over_groups(garm_group)
    each(owners - 1, lambda j: returning(j + 1).wait_send())


def write_out(*refs):
    copies = [pltpu.make_async_copy(refs[i], refs[3 + i], refs[6].at[i]) for i in range(3)]
    for copy in copies:
        copy.start()
    for copy in copies:
        copy.wait()


def per_device(owners, inner, garment, cotangent, body_points, stiffness, pair_garment, pair_body, pair_count):
    cap = pair_garment.shape[3]
    gb, bb = garment.shape[2] // BLOCK, body_points.shape[2] // BLOCK
    rows = 4 * cap
    vmem = pl.BlockSpec(memory_space=pltpu.VMEM)
    out_g, out_b, out_s = pl.pallas_call(
        functools.partial(kernel, owners, inner, cap, gb, bb),
        out_shape=(
            jax.ShapeDtypeStruct((3 * gb, BLOCK), F32),
            jax.ShapeDtypeStruct((3 * bb, BLOCK), F32),
            jax.ShapeDtypeStruct((bb, BLOCK), F32),
        ),
        in_specs=[pl.BlockSpec(memory_space=pltpu.HBM)] * 7,
        out_specs=[vmem] * 3,
        scratch_shapes=[
            pltpu.VMEM((3 * gb, BLOCK), F32),
            pltpu.VMEM((gb, BLOCK), F32),
            pltpu.VMEM((3 * bb, BLOCK), F32),
            pltpu.VMEM((bb, BLOCK), F32),
            pltpu.VMEM((cap, owners), jnp.int32),
            pltpu.VMEM((cap, owners), jnp.int32),
            pltpu.VMEM((1, owners), jnp.int32),
            pltpu.SemaphoreType.DMA((7,)),
            pltpu.VMEM((owners, 2 * BLOCK, 2 * BLOCK), BF),
            pltpu.VMEM((owners, 2 * BLOCK, 2 * BLOCK), BF),
            pltpu.VMEM((owners, rows, BLOCK), F32),
            pltpu.VMEM((owners, rows, BLOCK), F32),
            pltpu.VMEM((owners, rows + 1, BLOCK), F32),
            pltpu.VMEM((owners, rows + 1, BLOCK), F32),
            pltpu.VMEM((owners, 3 * cap, BLOCK), F32),
            pltpu.VMEM((owners, 3 * cap, BLOCK), F32),
            pltpu.VMEM((3 * 4 * bb, BLOCK), BF),
            pltpu.VMEM((owners // GROUP, 1, BLOCK), F32),
            pltpu.VMEM((owners, rows, BLOCK), F32),
            pltpu.VMEM((bb, BLOCK), F32),
            pltpu.VMEM((bb, BLOCK), F32),
            pltpu.SemaphoreType.DMA((owners,)),
            pltpu.SemaphoreType.DMA((owners,)),
            pltpu.SemaphoreType.DMA((owners,)),
            pltpu.SemaphoreType.DMA((owners,)),
            pltpu.SemaphoreType.DMA((2,)),
        ],
        compiler_params=pltpu.CompilerParams(collective_id=0, has_side_effects=True,
            vmem_limit_bytes=(8 * 2**20 + owners * 5 * 2**16)),
        name="contact",
    )(
        pltpu.with_memory_space_constraint(garment.reshape(3 * gb, BLOCK), pltpu.HBM),
        pltpu.with_memory_space_constraint(cotangent.reshape(gb, BLOCK), pltpu.HBM),
        pltpu.with_memory_space_constraint(body_points.reshape(3 * bb, BLOCK), pltpu.HBM),
        pltpu.with_memory_space_constraint(stiffness.reshape(bb, BLOCK), pltpu.HBM),
        pltpu.with_memory_space_constraint(pair_garment.reshape(owners, cap).T, pltpu.HBM),
        pltpu.with_memory_space_constraint(pair_body.reshape(owners, cap).T, pltpu.HBM),
        pltpu.with_memory_space_constraint(pair_count.reshape(1, owners), pltpu.HBM),
    )
    out_g, out_b, out_s = pl.pallas_call(
        write_out,
        out_shape=tuple(jax.ShapeDtypeStruct(o.shape, o.dtype) for o in (out_g, out_b, out_s)),
        in_specs=[vmem] * 3,
        out_specs=[pl.BlockSpec(memory_space=pltpu.HBM)] * 3,
        scratch_shapes=[pltpu.SemaphoreType.DMA((3,))],
        compiler_params=pltpu.CompilerParams(vmem_limit_bytes=2**20),
        name="write_out",
    )(out_g, out_b, out_s)
    return (
        out_g.reshape(1, 3, gb * BLOCK),
        out_b.reshape(1, 3, bb * BLOCK),
        out_s.reshape(bb * BLOCK),
    )


def solution(mesh):
    inner = mesh.shape["body"]
    owners = mesh.shape["garm"] * inner
    in_specs = (
        P(("grp", "frame"), None, ("garm", "body")),
        P(("grp", "frame"), ("garm", "body")),
        P(("grp", "frame"), None, ("garm", "body")),
        P(("grp", "garm", "body")),
        P(("grp", "frame"), ("garm", "body"), None, None),
        P(("grp", "frame"), ("garm", "body"), None, None),
        P(("grp", "frame"), ("garm", "body"), None),
    )
    out_specs = (
        P(("grp", "frame"), None, ("garm", "body")),
        P(("grp", "frame"), None, ("garm", "body")),
        P(("grp", "garm", "body")),
    )
    return jax.shard_map(
        functools.partial(per_device, owners, inner),
        mesh=mesh, in_specs=in_specs, out_specs=out_specs, check_vma=False)
```

profile of v0, /device:TPU:0, one launch (start us, length us, event | category | flops | bytes accessed | tf_op | source)
XLA Modules:
  0.0 17.2 jit_solution(10383944798595260742)
XLA Ops:
  0.6 15.9 %contact.1 = (f32[96,128]{1,0:T(8,128)S(1)}, f32[48,128]{1,0:T(8,128)S(1)}, f32[16,128]{1,0:T(8,128)S(1)}) custom-call(f32[96,128]{1,0:T(8,128)} %bitcast.14, f32[32,128]{1,0:T(8,128)} %bitcast.16, f32[48,128]{1,0:T(8,128)} %bitcast.15, f32[16,128]{1,0:T(8,128)} %bitcast.17, s32[4,8]{1,0:T(4,128)} %bitcast.18, s32[4,8]{1,0:T(4,128)} %bitcast.19, s32[1,8]{1,0:T(1,128)} %bitcast.20), custom_call_target="tpu_custom_call" | custom-call | tf_op jit(solution)/shard_map/contact/pallas_call | solution.py:256
  16.6 0.7 %write_out.1 = (f32[96,128]{1,0:T(8,128)}, f32[48,128]{1,0:T(8,128)}, f32[16,128]{1,0:T(8,128)}) custom-call(f32[96,128]{1,0:T(8,128)S(1)} %get-tuple-element.9.refs_0_, f32[48,128]{1,0:T(8,128)S(1)} %get-tuple-element.10.refs_1_, f32[16,128]{1,0:T(8,128)S(1)} %get-tuple-element.11.refs_2_), custom_call_target="tpu_custom_call" | custom-call | tf_op jit(solution)/shard_map/write_out/pallas_call | solution.py:305
where the time goes:
time: 17.4 us; the launch traced here: 17.2 us
  Pallas kernels  16.6 us (95%)
  between operations  0.64 us (4%)
    pallas_call x1, Pallas kernels, per_device(): pl.pallas_call(functools.partial(kernel, owners, inner, cap, gb, bb), out...  15.9 us
    pallas_call x1, Pallas kernels, per_device(): pl.pallas_call(write_out, out_shape=tuple((jax.ShapeDtypeStruct(o.shape,...  0.65 us

commit v1 on v0

--- a/solution.py
+++ b/solution.py
@@ -44,12 +44,17 @@
 
 def kernel(owners, inner, cap, gb, bb, *refs):
     hbm, refs = refs[:7], refs[7:]
-    (out_g, out_b, out_s, garm, cot, body, stiff, pg, pb, pc, isem, k_his, k_los, weights, bodies,
-     send, recv, rsend, rrecv, tab3, gtgt, parts, stl, strv,
-     ssem, rsem, rssem, rrsem, fsem) = refs
+    (out_g, out_b, out_s, garm, cot, btab, pg, pb, pc, isem, k_his, k_los, weights, bodies,
+     send, recv, rsend, rrecv, tab3, gtgt, parts, stl, strv, far,
+     ssem, rsem, rssem, rrsem, fsem, xsem, ysem, ready) = refs
     rows = 4 * cap
     outer_i, inner_i, frame_i = lax.axis_index("garm"), lax.axis_index("body"), lax.axis_index("frame")
     me = outer_i * inner + inner_i
+    outer = owners // inner
+    base = (outer - 2) * inner
+    last = range(base + inner, owners)
+    prior = range(base, base + inner)
+    first_row, last_row, head = outer_i == 0, outer_i == outer - 1, me == 0
 
     def peer(k):
         p, bit = me, 1
@@ -64,19 +69,36 @@
 
     barrier = pltpu.get_barrier_semaphore()
 
-    def greet(j):
-        pl.semaphore_signal(barrier, inc=1, device_id=device(owners - 1 - j), device_id_type=MESH)
+    groups = [1 << b for b in range(owners.bit_length() - 1)]
+
+    def below(bit):
+        return (me // bit) % 2 == 1
+
+    def over(first, count, cond, body):
+        pl.when(cond)(lambda: each(count, lambda j: body(first + j)))
+
+    def greet(k):
+        pl.semaphore_signal(barrier, inc=1, device_id=device(k), device_id_type=MESH)
+
+    def announce(k):
+        pl.semaphore_signal(ready.at[k], inc=1, device_id=device(k), device_id_type=MESH)
 
     loads = [
         pltpu.make_async_copy(src, dst, isem.at[i])
-        for i, (src, dst) in enumerate(zip(hbm, (garm, cot, body, stiff, pg, pb, pc)))]
+        for i, (src, dst) in enumerate(zip(
+            hbm, (garm, cot, btab.at[pl.ds(0, 3 * bb)], btab.at[pl.ds(3 * bb, bb)], pg, pb, pc)))]
     for load in loads:
         load.start()
-    each(owners - 1, greet)
+    for bit in reversed(groups):
+        over(bit, bit, jnp.logical_not(below(bit)), greet)
     pl.semaphore_signal(barrier, inc=1, device_id={"frame": 1 - frame_i}, device_id_type=MESH)
 
     for load in loads:
         load.wait()
+
+    pl.semaphore_wait(barrier, me + 1)
+    for bit in reversed(groups):
+        over(bit, bit, below(bit), announce)
 
     lane = lax.broadcasted_iota(jnp.int32, (1, BLOCK), 1)
     lane_q = lane % rows // cap
@@ -122,49 +144,69 @@
             src_ref=rsend.at[peer(k)], dst_ref=rrecv.at[me], send_sem=rssem.at[k], recv_sem=rrsem.at[k],
             device_id=device(k), device_id_type=MESH)
 
-    tab3[...] = jnp.concatenate(
-        split3(jnp.concatenate([body[...] * SCALE, stiff[...]], axis=0)), axis=0)
-
-    row_c = lax.broadcasted_iota(jnp.int32, (rows, BLOCK), 0) % cap
+    def table(rows_in):
+        return jnp.concatenate(
+            split3(jnp.concatenate([rows_in[: 3 * bb] * SCALE, rows_in[3 * bb :]], axis=0)), axis=0)
+
+    def pushing(k):
+        return pltpu.make_async_remote_copy(
+            src_ref=btab, dst_ref=far.at[k - base], send_sem=xsem.at[k - base],
+            recv_sem=ysem.at[k - base], device_id=device(k), device_id_type=MESH)
+
+    tab3[...] = table(btab[...])
+
+    row_id = lax.broadcasted_iota(jnp.int32, (rows, BLOCK), 0)
+    row_c, place = row_id % cap, row_id < 3 * cap
     low_i, low_j = row_c < 2, row_c % 2 == 0
     wide = lax.broadcasted_iota(jnp.int32, (rows, 3 * 4 * bb), 1) % (4 * bb)
+    slots = [jnp.concatenate([jnp.where(row_c == c, 1.0, 0.0).astype(BF)] * 6, axis=0) for c in range(cap)]
 
     def lhs(x, low):
         both = jnp.concatenate([jnp.where(low, x, 0.0), jnp.where(low, 0.0, x)], axis=1)
         return jnp.concatenate(split3(both), axis=0)
 
-    def process(k, got, row):
-        turned = jnp.transpose(jnp.concatenate([got, row, jnp.zeros((7, BLOCK), F32)], axis=0))
-        target = turned[:rows, rows : rows + 1]
-        onehot = jnp.where(wide == target.astype(jnp.int32), 1.0, 0.0).astype(BF)
-        part = dot(onehot, tab3[...])
-        kernels = []
-        for c in range(cap):
-            dist = None
-            for q in range(3):
-                r = q * cap + c
-                delta = turned[:, r : r + 1] - part[r : r + 1, :]
-                dist = delta * delta if dist is None else dist + delta * delta
-            kernels.append(jnp.exp2(-dist))
+    def terms(x, scale):
+        square = x[: 3 * cap] * x[: 3 * cap]
+        norm = square[:cap] + square[cap : 2 * cap] + square[2 * cap :]
+        full = jnp.concatenate([x[: 3 * cap] * scale, -norm], axis=0)
+        hi = full.astype(BF).astype(F32)
+        mid = (full - hi).astype(BF).astype(F32)
+        low = full - hi - mid
+        return [t.astype(BF) for t in (hi, mid, low, jnp.where(place, hi, 1.0), jnp.where(place, mid, 1.0))]
+
+    def evaluate(got, row, tab):
+        turned = jnp.transpose(jnp.concatenate([row, jnp.zeros((7, BLOCK), F32)], axis=0))
+        onehot = jnp.where(wide == turned[:rows, 0:1].astype(jnp.int32), 1.0, 0.0).astype(BF)
+        part = dot(onehot, tab)
+        a1, a2, a3, a1o, a2o = terms(got, 1.0)
+        b1, b2, b3, b1o, b2o = terms(part, 2.0)
+        left = jnp.concatenate([a1, a2, a3, a2o, a1o, a1o], axis=0)
+        right = jnp.concatenate([b1o, b2o, b1o, b1, b2, b3], axis=0)
         square = jnp.concatenate(
-            [jnp.concatenate(kernels[0:2], axis=1), jnp.concatenate(kernels[2:4], axis=1)], axis=0)
+            [jnp.exp2(lax.dot_general(
+                left, jnp.concatenate([right * slots[c], right * slots[c + 1]], axis=1),
+                (((0,), (0,)), ((), ())), preferred_element_type=F32)) for c in (0, 2)], axis=0)
         k_hi = square.astype(BF)
-        k_lo = (square - k_hi.astype(F32)).astype(BF)
+        return part, k_hi, (square - k_hi.astype(F32)).astype(BF)
+
+    def pull(got, part, k_hi, k_lo):
         cots = got[3 * cap :]
         stf = part[3 * cap :]
-        w = jnp.concatenate([jnp.concatenate([cots] * 3, axis=0) * got[: 3 * cap], cots], axis=0)
-        v = jnp.concatenate([jnp.concatenate([stf] * 3, axis=0) * part[: 3 * cap], stf], axis=0)
-
-        k_his[k], k_los[k] = k_hi, k_lo
-        weights[k] = w
-        bodies[k] = part
-        lv = lhs(v, low_j)
+        lv = lhs(jnp.concatenate([jnp.concatenate([stf] * 3, axis=0) * part[: 3 * cap], stf], axis=0), low_j)
         rg = dot_t(lv, k_hi) + dot_t(lv, k_lo)
         rg = rg[:rows] + rg[rows : 2 * rows] + rg[2 * rows :]
         rg = jnp.where(low_i, rg[:, :BLOCK], rg[:, BLOCK:])
         sums = jnp.concatenate([rg[3 * cap :]] * 3, axis=0)
         cots3 = jnp.concatenate([cots] * 3, axis=0)
         return GRAD * (cots3 * (got[: 3 * cap] * sums - rg[: 3 * cap]))
+
+    def process(k, got, row):
+        part, k_hi, k_lo = evaluate(got, row, tab3[...])
+        cots = got[3 * cap :]
+        k_his[k], k_los[k] = k_hi, k_lo
+        weights[k] = jnp.concatenate([jnp.concatenate([cots] * 3, axis=0) * got[: 3 * cap], cots], axis=0)
+        bodies[k] = part
+        return pull(got, part, k_hi, k_lo)
 
     def finish(k):
         part = bodies[k]
@@ -178,12 +220,41 @@
         body_grad = GRAD * (stf3 * (part[: 3 * cap] * cols3 - rb[: 3 * cap]))
         parts[k] = jnp.concatenate([body_grad, amplitude * cols], axis=0)
 
+    for bit in reversed(groups):
+        over(bit, bit, below(bit), lambda k: outgoing(k).start())
+
+    def push_last():
+        for k in last:
+            pushing(k).start()
+
+    def push_prior():
+        pushing(me).start()
+
+    pl.when(last_row)(push_last)
+    pl.when(outer_i == outer - 2)(push_prior)
+
+    def raise_to(first, count, bit):
+        def one(k):
+            pl.semaphore_wait(ready.at[k], 1)
+            outgoing(k).start()
+
+        over(first, count, jnp.logical_not(below(bit)), one)
+
     recv[me, pl.ds(rows, 1), :] = send[me, pl.ds(rows, 1), :]
     rrecv[me] = process(me, send[me, pl.ds(0, rows), :], send[me, pl.ds(rows, 1), :])
 
-    pl.semaphore_wait(barrier, owners)
-    each(owners - 1, lambda j: outgoing(owners - 1 - j).start())
-
+
+    def returns(k):
+        if not isinstance(k, int):
+            here = jnp.logical_or(k < base, jnp.logical_and(k < base + inner, me != k))
+            return jnp.logical_or(here, jnp.logical_and(k >= base + inner, jnp.logical_not(last_row)))
+        return True if k < base else (me != k if k in prior else jnp.logical_not(last_row))
+
+    def when(cond, body):
+        if cond is True:
+            body()
+        else:
+            pl.when(cond)(body)
 
     def arrive(ks):
         for k in ks:
@@ -192,10 +263,26 @@
                  for k in ks]
         for k, grad in zip(ks, grads):
             rsend[peer(k)] = grad
-            returning(k).start()
-
+        for k in ks:
+            when(returns(k), lambda k=k: returning(k).start())
+
+    for bit in groups[:-1]:
+        raise_to(bit, bit, bit)
+    raise_to(owners // 2, base + inner - owners // 2, owners // 2)
     arrive([1])
+    raise_to(base + inner, inner, owners // 2)
     each(owners // 2 - 1, lambda j: arrive([2 * j + 2, 2 * j + 3]))
+
+    def fetch(ks):
+        for k in ks:
+            pushing(k).wait_recv()
+        done = []
+        for k in ks:
+            got, row = send[peer(k), pl.ds(0, rows), :], send[peer(k), pl.ds(rows, 1), :]
+            done.append(pull(got, *evaluate(got, row, table(far[k - base]))))
+        for k, grad in zip(ks, done):
+            rrecv[peer(k)] = grad
+
     each(owners, finish)
 
     def scatter(height, target_row, values):
@@ -224,10 +311,19 @@
         device_id={"frame": 1 - frame_i}, device_id_type=MESH)
     stiff_copy.start()
     out_b[...] = body_sum[: 3 * bb]
+    pl.when(head)(lambda: fetch([*prior, *last]))
+    pl.when(jnp.logical_and(first_row, jnp.logical_not(head)))(lambda: fetch(last))
     each(owners - 1, lambda j: outgoing(j + 1).wait_send())
     stiff_copy.wait()
     out_s[...] = stl[...] + strv[...]
-    each(owners - 1, lambda j: returning(j + 1).wait_recv())
+    each(base - 1, lambda j: returning(j + 1).wait_recv())
+
+    def await_returns(ks):
+        for k in ks:
+            returning(k).wait_recv()
+
+    pl.when(jnp.logical_not(head))(lambda: await_returns(prior))
+    pl.when(jnp.logical_not(first_row))(lambda: await_returns(last))
 
     def garm_group(u):
         blank = jnp.zeros((cap, BLOCK), F32)
@@ -237,7 +333,17 @@
         return scatter(3 * gb, gtgt[u].astype(jnp.int32), jnp.concatenate(pieces, axis=0))
 
     out_g[...] = over_groups(garm_group)
-    each(owners - 1, lambda j: returning(j + 1).wait_send())
+    each(owners - 1, lambda j: when(returns(j + 1), lambda: returning(j + 1).wait_send()))
+
+    def settle_last():
+        for k in last:
+            pushing(k).wait_send()
+
+    def settle_prior():
+        pushing(me).wait_send()
+
+    pl.when(last_row)(settle_last)
+    pl.when(outer_i == outer - 2)(settle_prior)
 
 
 def write_out(*refs):
@@ -265,8 +371,7 @@
         scratch_shapes=[
             pltpu.VMEM((3 * gb, BLOCK), F32),
             pltpu.VMEM((gb, BLOCK), F32),
-            pltpu.VMEM((3 * bb, BLOCK), F32),
-            pltpu.VMEM((bb, BLOCK), F32),
+            pltpu.VMEM((4 * bb, BLOCK), F32),
             pltpu.VMEM((cap, owners), jnp.int32),
             pltpu.VMEM((cap, owners), jnp.int32),
             pltpu.VMEM((1, owners), jnp.int32),
@@ -284,11 +389,15 @@
             pltpu.VMEM((owners, rows, BLOCK), F32),
             pltpu.VMEM((bb, BLOCK), F32),
             pltpu.VMEM((bb, BLOCK), F32),
+            pltpu.VMEM((2 * inner, 4 * bb, BLOCK), F32),
             pltpu.SemaphoreType.DMA((owners,)),
             pltpu.SemaphoreType.DMA((owners,)),
             pltpu.SemaphoreType.DMA((owners,)),
             pltpu.SemaphoreType.DMA((owners,)),
             pltpu.SemaphoreType.DMA((2,)),
+            pltpu.SemaphoreType.DMA((2 * inner,)),
+            pltpu.SemaphoreType.DMA((2 * inner,)),
+            pltpu.SemaphoreType.REGULAR((owners,)),
         ],
         compiler_params=pltpu.CompilerParams(collective_id=0, has_side_effects=True,
             vmem_limit_bytes=(8 * 2**20 + owners * 5 * 2**16)),

time: 17.4 us -> 14.9 us (0.86)
  the two profiles are of different devices: /device:TPU:0 before, /device:TPU:10 now
where the time goes in v1:
time: 14.9 us; the launch traced here: 14.7 us
  Pallas kernels  14.1 us (95%)
  between operations  0.64 us (4%)
    pallas_call x1, Pallas kernels, per_device(): pl.pallas_call(functools.partial(kernel, owners, inner, cap, gb, bb), out...  13.4 us
    pallas_call x1, Pallas kernels, per_device(): pl.pallas_call(write_out, out_shape=tuple((jax.ShapeDtypeStruct(o.shape,...  0.65 us

profile of v1, /device:TPU:10, one launch (start us, length us, event | category | flops | bytes accessed | tf_op | source)
XLA Modules:
  0.0 14.7 jit_solution(10113903015891205324)
XLA Ops:
  0.6 13.4 %contact.1 = (f32[96,128]{1,0:T(8,128)S(1)}, f32[48,128]{1,0:T(8,128)S(1)}, f32[16,128]{1,0:T(8,128)S(1)}) custom-call(f32[96,128]{1,0:T(8,128)} %bitcast.14, f32[32,128]{1,0:T(8,128)} %bitcast.16, f32[48,128]{1,0:T(8,128)} %bitcast.15, f32[16,128]{1,0:T(8,128)} %bitcast.17, s32[4,8]{1,0:T(4,128)} %bitcast.18, s32[4,8]{1,0:T(4,128)} %bitcast.19, s32[1,8]{1,0:T(1,128)} %bitcast.20), custom_call_target="tpu_custom_call" | custom-call | tf_op jit(solution)/shard_map/contact/pallas_call | solution.py:362
  14.0 0.7 %write_out.1 = (f32[96,128]{1,0:T(8,128)}, f32[48,128]{1,0:T(8,128)}, f32[16,128]{1,0:T(8,128)}) custom-call(f32[96,128]{1,0:T(8,128)S(1)} %get-tuple-element.9.refs_0_, f32[48,128]{1,0:T(8,128)S(1)} %get-tuple-element.10.refs_1_, f32[16,128]{1,0:T(8,128)S(1)} %get-tuple-element.11.refs_2_), custom_call_target="tpu_custom_call" | custom-call | tf_op jit(solution)/shard_map/write_out/pallas_call | solution.py:414

commit v2 on v1

--- a/solution.py
+++ b/solution.py
@@ -75,7 +75,7 @@
         return (me // bit) % 2 == 1
 
     def over(first, count, cond, body):
-        pl.when(cond)(lambda: each(count, lambda j: body(first + j)))
+        pl.when(cond)(lambda: each(count, lambda j: body(first + count - 1 - j)))
 
     def greet(k):
         pl.semaphore_signal(barrier, inc=1, device_id=device(k), device_id_type=MESH)
@@ -87,18 +87,20 @@
         pltpu.make_async_copy(src, dst, isem.at[i])
         for i, (src, dst) in enumerate(zip(
             hbm, (garm, cot, btab.at[pl.ds(0, 3 * bb)], btab.at[pl.ds(3 * bb, bb)], pg, pb, pc)))]
-    for load in loads:
+    for load in loads[4:] + loads[:4]:
         load.start()
     for bit in reversed(groups):
         over(bit, bit, jnp.logical_not(below(bit)), greet)
     pl.semaphore_signal(barrier, inc=1, device_id={"frame": 1 - frame_i}, device_id_type=MESH)
 
-    for load in loads:
+    def meet():
+        pl.semaphore_wait(barrier, me + 1)
+        for bit in reversed(groups):
+            over(bit, bit, below(bit), announce)
+
+    pl.when(inner_i == inner - 1)(meet)
+    for load in loads[4:]:
         load.wait()
-
-    pl.semaphore_wait(barrier, me + 1)
-    for bit in reversed(groups):
-        over(bit, bit, below(bit), announce)
 
     lane = lax.broadcasted_iota(jnp.int32, (1, BLOCK), 1)
     lane_q = lane % rows // cap
@@ -116,10 +118,9 @@
     full_b = full[:, BLOCK : 2 * BLOCK] + (lane_q * bb).astype(F32)
     live = jnp.where(
         (lane_q < 3) | ((lane % cap).astype(F32) < full[:, 2 * BLOCK :]), 1.0, 0.0)
-    gtab = jnp.concatenate(
-        split3(jnp.concatenate([garm[...] * SCALE, cot[...]], axis=0)), axis=0)
     own = lax.broadcasted_iota(jnp.int32, (GROUP, BLOCK), 0) == lane // rows
     wide_g = lax.broadcasted_iota(jnp.int32, (BLOCK, 12 * gb), 1) % (4 * gb)
+    picks = []
     for u in range(owners // GROUP):
         here = slice(u * GROUP, (u + 1) * GROUP)
         targets = jnp.sum(jnp.where(own, full_g[here], 0.0), axis=0, keepdims=True)
@@ -127,12 +128,19 @@
         gtgt[u] = targets
         turned = jnp.transpose(
             jnp.concatenate([targets, lives, jnp.zeros((6, BLOCK), F32)], axis=0))
-        hot = jnp.where(wide_g == turned[:, 0:1].astype(jnp.int32), 1.0, 0.0).astype(BF)
-        chosen = dot(hot, gtab) * turned[:, 1:2]
+        picks.append((jnp.where(wide_g == turned[:, 0:1].astype(jnp.int32), 1.0, 0.0).astype(BF), turned[:, 1:2]))
+    for d in range(owners):
+        send[d, pl.ds(rows, 1), :] = full_b[d : d + 1]
+
+    pl.when(inner_i < inner - 1)(meet)
+    for load in loads[:2]:
+        load.wait()
+    gtab = jnp.concatenate(
+        split3(jnp.concatenate([garm[...] * SCALE, cot[...]], axis=0)), axis=0)
+    for u, (hot, lives) in enumerate(picks):
+        chosen = dot(hot, gtab) * lives
         for m in range(GROUP):
             send[u * GROUP + m, pl.ds(0, rows), :] = chosen[m * rows : (m + 1) * rows]
-    for d in range(owners):
-        send[d, pl.ds(rows, 1), :] = full_b[d : d + 1]
 
     def outgoing(k):
         return pltpu.make_async_remote_copy(
@@ -153,7 +161,6 @@
             src_ref=btab, dst_ref=far.at[k - base], send_sem=xsem.at[k - base],
             recv_sem=ysem.at[k - base], device_id=device(k), device_id_type=MESH)
 
-    tab3[...] = table(btab[...])
 
     row_id = lax.broadcasted_iota(jnp.int32, (rows, BLOCK), 0)
     row_c, place = row_id % cap, row_id < 3 * cap
@@ -221,7 +228,10 @@
         parts[k] = jnp.concatenate([body_grad, amplitude * cols], axis=0)
 
     for bit in reversed(groups):
-        over(bit, bit, below(bit), lambda k: outgoing(k).start())
+        pl.when(below(bit))(lambda bit=bit: each(bit, lambda j: outgoing(bit + j).start()))
+    for load in loads[2:4]:
+        load.wait()
+    tab3[...] = table(btab[...])
 
     def push_last():
         for k in last:
@@ -230,18 +240,19 @@
     def push_prior():
         pushing(me).start()
 
-    pl.when(last_row)(push_last)
     pl.when(outer_i == outer - 2)(push_prior)
 
     def raise_to(first, count, bit):
-        def one(k):
-            pl.semaphore_wait(ready.at[k], 1)
-            outgoing(k).start()
-
-        over(first, count, jnp.logical_not(below(bit)), one)
+        def one(j):
+            pl.semaphore_wait(ready.at[first + j], 1)
+            outgoing(first + j).start()
+
+        pl.when(jnp.logical_not(below(bit)))(lambda: each(count, one))
 
     recv[me, pl.ds(rows, 1), :] = send[me, pl.ds(rows, 1), :]
     rrecv[me] = process(me, send[me, pl.ds(0, rows), :], send[me, pl.ds(rows, 1), :])
+
+    pl.when(last_row)(push_last)
 
 
     def returns(k):
@@ -268,9 +279,12 @@
 
     for bit in groups[:-1]:
         raise_to(bit, bit, bit)
-    raise_to(owners // 2, base + inner - owners // 2, owners // 2)
+    half = owners // 2
+    odd = below(half // 2)
+    pl.when(odd)(lambda: raise_to(half + half // 2, half // 2, half))
+    raise_to(half, half // 2, half)
     arrive([1])
-    raise_to(base + inner, inner, owners // 2)
+    pl.when(jnp.logical_not(odd))(lambda: raise_to(half + half // 2, half // 2, half))
     each(owners // 2 - 1, lambda j: arrive([2 * j + 2, 2 * j + 3]))
 
     def fetch(ks):

time: 14.9 us -> 14.6 us (0.980)
  the two profiles are of different devices: /device:TPU:10 before, /device:TPU:0 now
where the time goes in v2:
time: 14.6 us; the launch traced here: 14.4 us
  Pallas kernels  13.7 us (94%)
  between operations  0.64 us (4%)
    pallas_call x1, Pallas kernels, per_device(): pl.pallas_call(functools.partial(kernel, owners, inner, cap, gb, bb), out...  13.1 us
    pallas_call x1, Pallas kernels, per_device(): pl.pallas_call(write_out, out_shape=tuple((jax.ShapeDtypeStruct(o.shape,...  0.65 us

profile of v2, /device:TPU:0, one launch (start us, length us, event | category | flops | bytes accessed | tf_op | source)
XLA Modules:
  0.0 14.4 jit_solution(17778416742912789)
XLA Ops:
  0.6 13.1 %contact.1 = (f32[96,128]{1,0:T(8,128)S(1)}, f32[48,128]{1,0:T(8,128)S(1)}, f32[16,128]{1,0:T(8,128)S(1)}) custom-call(f32[96,128]{1,0:T(8,128)} %bitcast.14, f32[32,128]{1,0:T(8,128)} %bitcast.16, f32[48,128]{1,0:T(8,128)} %bitcast.15, f32[16,128]{1,0:T(8,128)} %bitcast.17, s32[4,8]{1,0:T(4,128)} %bitcast.18, s32[4,8]{1,0:T(4,128)} %bitcast.19, s32[1,8]{1,0:T(1,128)} %bitcast.20), custom_call_target="tpu_custom_call" | custom-call | tf_op jit(solution)/shard_map/contact/pallas_call | solution.py:376
  13.7 0.7 %write_out.1 = (f32[96,128]{1,0:T(8,128)}, f32[48,128]{1,0:T(8,128)}, f32[16,128]{1,0:T(8,128)}) custom-call(f32[96,128]{1,0:T(8,128)S(1)} %get-tuple-element.9.refs_0_, f32[48,128]{1,0:T(8,128)S(1)} %get-tuple-element.10.refs_1_, f32[16,128]{1,0:T(8,128)S(1)} %get-tuple-element.11.refs_2_), custom_call_target="tpu_custom_call" | custom-call | tf_op jit(solution)/shard_map/write_out/pallas_call | solution.py:428

commit v3 on v2

--- a/solution.py
+++ b/solution.py
@@ -116,23 +116,24 @@
         preferred_element_type=F32)
     full_g = full[:, :BLOCK] + (lane_q * gb).astype(F32)
     full_b = full[:, BLOCK : 2 * BLOCK] + (lane_q * bb).astype(F32)
-    live = jnp.where(
-        (lane_q < 3) | ((lane % cap).astype(F32) < full[:, 2 * BLOCK :]), 1.0, 0.0)
     own = lax.broadcasted_iota(jnp.int32, (GROUP, BLOCK), 0) == lane // rows
     wide_g = lax.broadcasted_iota(jnp.int32, (BLOCK, 12 * gb), 1) % (4 * gb)
     picks = []
+    tall = jnp.concatenate([pg[...].astype(F32)] * (BLOCK // cap), axis=0)
+    tall_n = jnp.broadcast_to(pc[...].astype(F32), (BLOCK, owners))
+    down = lax.broadcasted_iota(jnp.int32, (BLOCK, owners), 0)
+    across = lax.broadcasted_iota(jnp.int32, (BLOCK, owners), 1)
+    down_q = lax.broadcasted_iota(jnp.int32, (BLOCK, 1), 0) % rows // cap
+    down_c = lax.broadcasted_iota(jnp.int32, (BLOCK, 1), 0) % cap
     for u in range(owners // GROUP):
         here = slice(u * GROUP, (u + 1) * GROUP)
-        targets = jnp.sum(jnp.where(own, full_g[here], 0.0), axis=0, keepdims=True)
-        lives = jnp.sum(jnp.where(own, live[here], 0.0), axis=0, keepdims=True)
-        gtgt[u] = targets
-        turned = jnp.transpose(
-            jnp.concatenate([targets, lives, jnp.zeros((6, BLOCK), F32)], axis=0))
-        picks.append((jnp.where(wide_g == turned[:, 0:1].astype(jnp.int32), 1.0, 0.0).astype(BF), turned[:, 1:2]))
-    for d in range(owners):
-        send[d, pl.ds(rows, 1), :] = full_b[d : d + 1]
-
-    pl.when(inner_i < inner - 1)(meet)
+        gtgt[u] = jnp.sum(jnp.where(own, full_g[here], 0.0), axis=0, keepdims=True)
+        mine = across == down // rows + u * GROUP
+        block = jnp.sum(jnp.where(mine, tall, 0.0), axis=1, keepdims=True).astype(jnp.int32) + down_q * gb
+        count = jnp.sum(jnp.where(mine, tall_n, 0.0), axis=1, keepdims=True)
+        lives = jnp.where((down_q < 3) | (down_c.astype(F32) < count), 1.0, 0.0)
+        picks.append((jnp.where(wide_g == block, 1.0, 0.0).astype(BF), lives))
+
     for load in loads[:2]:
         load.wait()
     gtab = jnp.concatenate(
@@ -141,6 +142,9 @@
         chosen = dot(hot, gtab) * lives
         for m in range(GROUP):
             send[u * GROUP + m, pl.ds(0, rows), :] = chosen[m * rows : (m + 1) * rows]
+    for d in range(owners):
+        send[d, pl.ds(rows, 1), :] = full_b[d : d + 1]
+    pl.when(inner_i < inner - 1)(meet)
 
     def outgoing(k):
         return pltpu.make_async_remote_copy(

time: 14.6 us -> 14.4 us (0.986)
    pallas_call x1, Pallas kernels: 13.1 us -> 12.9 us  [per_device(): pl.pallas_call(functools.partial(kernel, owners, inner, cap, gb, bb), out...]
where the time goes in v3:
time: 14.4 us; the launch traced here: 14.2 us
  Pallas kernels  13.6 us (94%)
  between operations  0.64 us (4%)
    pallas_call x1, Pallas kernels, per_device(): pl.pallas_call(functools.partial(kernel, owners, inner, cap, gb, bb), out...  12.9 us
    pallas_call x1, Pallas kernels, per_device(): pl.pallas_call(write_out, out_shape=tuple((jax.ShapeDtypeStruct(o.shape,...  0.65 us

profile of v3, /device:TPU:0, one launch (start us, length us, event | category | flops | bytes accessed | tf_op | source)
XLA Modules:
  0.0 14.2 jit_solution(9270191703730528578)
XLA Ops:
  0.6 12.9 %contact.1 = (f32[96,128]{1,0:T(8,128)S(1)}, f32[48,128]{1,0:T(8,128)S(1)}, f32[16,128]{1,0:T(8,128)S(1)}) custom-call(f32[96,128]{1,0:T(8,128)} %bitcast.14, f32[32,128]{1,0:T(8,128)} %bitcast.16, f32[48,128]{1,0:T(8,128)} %bitcast.15, f32[16,128]{1,0:T(8,128)} %bitcast.17, s32[4,8]{1,0:T(4,128)} %bitcast.18, s32[4,8]{1,0:T(4,128)} %bitcast.19, s32[1,8]{1,0:T(1,128)} %bitcast.20), custom_call_target="tpu_custom_call" | custom-call | tf_op jit(solution)/shard_map/contact/pallas_call | solution.py:380
  13.6 0.7 %write_out.1 = (f32[96,128]{1,0:T(8,128)}, f32[48,128]{1,0:T(8,128)}, f32[16,128]{1,0:T(8,128)}) custom-call(f32[96,128]{1,0:T(8,128)S(1)} %get-tuple-element.9.refs_0_, f32[48,128]{1,0:T(8,128)S(1)} %get-tuple-element.10.refs_1_, f32[16,128]{1,0:T(8,128)S(1)} %get-tuple-element.11.refs_2_), custom_call_target="tpu_custom_call" | custom-call | tf_op jit(solution)/shard_map/write_out/pallas_call | solution.py:432
